TPU v7x, 32 devices: a whole 2x2x4 slice. The times are simulated.
32 devices in a mesh: cell: 4 (over y, x), sub: 8 (over z, core).
Axes of the slice: x: 2, y: 2, z: 4, core: 2. Of those that a mesh axis runs over, the one named last changes fastest.
Arguments:
- shell_conc: float32 [4, 32, 10, 128, 128], P('cell', 'sub'), may hold values from 0.2 to 0.8
- heat_rise: float32 [4, 30, 128, 128], P('cell', None, 'sub'), may hold values from -5 to 5
- layer_current: float32 [4, 32, 128, 128], P('cell', 'sub'), may hold values from -4 to 4
- layer_counts: int32 [8], replicated, may hold values from 1 to 4, 30 in all
- contacts: int32 [4, 2], replicated, may hold values from -1 to 3, as said below
Outputs:
- conc_new: float32 [4, 32, 10, 128, 128], P('cell', 'sub')
- heat_new: float32 [4, 30, 128, 128], P('cell', None, 'sub')
Inputs may be any that keep to these rules, and one draw needn't show every extreme that they name: `layer_counts`: entry d is the number of consecutive layers held by index d of sub, in order; the entries sum to 30 and the largest is exactly 4. `contacts`: row c names the cell below and the cell above cell c in one stacking order of all 4 cells, each cell once; -1 marks the two ends of the stack.
All inputs are finite; a program needn't handle non-finite values.
Results may differ from a plain program's by a relative error of at most 0.0003.
Values sent between devices are 32-bit elements; how exact they have to be, the bound alone decides.
A program may use at most 64 MiB of HBM per device.

v0:
```python
import jax
import jax.numpy as jnp
from jax import lax
from jax.sharding import PartitionSpec as P

BASE_KELVIN = 298.15
RATE_ACTIVATION = 5000.0
DIFFUSION_ACTIVATION = 3000.0
RATE_CONSTANT = 0.5
VOLT_PER_KELVIN = 2.0 * 8.314462618 / 96485.33212
HEAT_SCALE = 10.0
ENTROPY_SLOPE = 0.001
DIFFUSION_STEP = 0.005
SURFACE_STEP = 0.005
INPLANE_CONDUCT = 0.25
THROUGH_CONDUCT = 2.0
CONTACT_CONDUCT = 0.5


def with_halo(cells, sides, width):
    for axis, dim in sides:
        count = lax.axis_size(axis)
        ends = count - 1
        head = lax.slice_in_dim(cells, 0, width, axis=dim)
        tail = lax.slice_in_dim(cells, cells.shape[dim] - width, cells.shape[dim], axis=dim)
        cells = jnp.concatenate(
            [
                lax.ppermute(tail, axis, [(i, (i + 1) % count) for i in range(ends)]),
                cells,
                lax.ppermute(head, axis, [((i + 1) % count, i) for i in range(ends)]),
            ],
            axis=dim,
        )
    return cells


def inverse_sine(value):
    magnitude = jnp.abs(value)
    rooted = jnp.sqrt(1.0 + magnitude * magnitude)
    positive = jnp.log1p(magnitude + magnitude * magnitude / (1.0 + rooted))
    return jnp.where(value < 0.0, -positive, positive)


def layer_tables(layer_counts, slot_count, layer_total):
    finish = jnp.cumsum(layer_counts)
    starts = finish - layer_counts
    devices = layer_counts.shape[0]
    device_ids = jnp.arange(devices, dtype=jnp.int32)
    slot_index = jnp.arange(devices * slot_count, dtype=jnp.int32)
    slot_owner = slot_index // slot_count
    slot_place = slot_index % slot_count
    owner_hits = slot_owner[:, None] == device_ids[None, :]
    owner_count = jnp.sum(jnp.where(owner_hits, layer_counts[None, :], 0), axis=1)
    owner_start = jnp.sum(jnp.where(owner_hits, starts[None, :], 0), axis=1)
    live_slot = slot_place < owner_count
    slot_layer = jnp.minimum(owner_start + slot_place, layer_total - 1)
    layer_index = jnp.arange(layer_total, dtype=jnp.int32)
    layer_owner = jnp.sum((finish[None, :] <= layer_index[:, None]).astype(jnp.int32), axis=1)
    layer_hits = layer_owner[:, None] == device_ids[None, :]
    layer_start = jnp.sum(jnp.where(layer_hits, starts[None, :], 0), axis=1)
    layer_slot = layer_owner * slot_count + layer_index - layer_start
    return (live_slot, slot_layer, layer_slot)


def kinetics(surface, kelvin, current):
    reciprocal = 1.0 / BASE_KELVIN - 1.0 / kelvin
    base_rate = (
        RATE_CONSTANT * jnp.exp(RATE_ACTIVATION * reciprocal) * jnp.sqrt(surface * (1.0 - surface))
    )
    ratio_rate = current / (2.0 * base_rate)
    arcsine = inverse_sine(ratio_rate)
    overvoltage = VOLT_PER_KELVIN * kelvin * arcsine
    entropic = ENTROPY_SLOPE * (0.5 - surface)
    source = HEAT_SCALE * current * (overvoltage + kelvin * entropic)
    heat_slope = (
        HEAT_SCALE
        * current
        * (
            VOLT_PER_KELVIN * arcsine
            - VOLT_PER_KELVIN
            * ratio_rate
            * RATE_ACTIVATION
            / (kelvin * jnp.sqrt(1.0 + ratio_rate * ratio_rate))
            + entropic
        )
    )
    return (source, heat_slope)


def particle(states, kelvin, current):
    shells = states.shape[1]
    speedup = jnp.exp(DIFFUSION_ACTIVATION * (1.0 / BASE_KELVIN - 1.0 / kelvin))
    volumes = [((radial + 1) ** 3 - radial**3) / (3.0 * shells**3) for radial in range(shells)]
    linkage = [
        DIFFUSION_STEP * speedup * ((radial + 1) ** 2 / shells**2 * shells)
        for radial in range(shells - 1)
    ]
    uppers = []
    values = []
    for radial in range(shells):
        diagonal = volumes[radial] + jnp.zeros_like(kelvin)
        right_side = volumes[radial] * states[:, radial]
        if radial < shells - 1:
            diagonal = diagonal + linkage[radial]
        else:
            right_side = right_side - SURFACE_STEP * current
        if radial > 0:
            diagonal = diagonal + linkage[radial - 1] - linkage[radial - 1] * uppers[radial - 1]
            right_side = right_side + linkage[radial - 1] * values[radial - 1]
        if radial < shells - 1:
            uppers.append(linkage[radial] / diagonal)
        else:
            uppers.append(jnp.zeros_like(kelvin))
        values.append(right_side / diagonal)
    result = [None] * shells
    result[shells - 1] = values[shells - 1]
    for radial in range(shells - 2, -1, -1):
        result[radial] = values[radial] + uppers[radial] * result[radial + 1]
    return jnp.stack(result, axis=1)


def column_solve(right_side, heat_slope):
    layer_total = right_side.shape[1]
    uppers = []
    values = []
    for height in range(layer_total):
        diagonal = 1.0 - heat_slope[:, height]
        source = right_side[:, height]
        if height > 0:
            diagonal = diagonal + THROUGH_CONDUCT - THROUGH_CONDUCT * uppers[height - 1]
            source = source + THROUGH_CONDUCT * values[height - 1]
        if height < layer_total - 1:
            diagonal = diagonal + THROUGH_CONDUCT
        uppers.append(THROUGH_CONDUCT / diagonal)
        values.append(source / diagonal)
    result = [None] * layer_total
    result[layer_total - 1] = values[layer_total - 1]
    for height in range(layer_total - 2, -1, -1):
        result[height] = values[height] + uppers[height] * result[height + 1]
    return jnp.stack(result, axis=1)


def per_device(shell_conc, heat_rise, layer_current, layer_counts, contacts):
    slot_count = shell_conc.shape[1]
    shells = shell_conc.shape[2]
    layer_total = heat_rise.shape[1]
    live_slot, slot_layer, layer_slot = layer_tables(layer_counts, slot_count, layer_total)
    position = lax.axis_index("sub")
    devices = lax.axis_size("sub")
    outgoing = jnp.take(heat_rise, slot_layer, axis=1)
    slot_rise = lax.all_to_all(outgoing, "sub", split_axis=1, concat_axis=2, tiled=True)
    kelvin = BASE_KELVIN + slot_rise
    surface = shell_conc[:, :, shells - 1]
    source, heat_slope = kinetics(surface, kelvin, layer_current)
    got_source, got_slope = (
        lax.all_to_all(source, "sub", split_axis=2, concat_axis=1, tiled=True),
        lax.all_to_all(heat_slope, "sub", split_axis=2, concat_axis=1, tiled=True),
    )
    layer_source = jnp.take(got_source, layer_slot, axis=1)
    layer_slope = jnp.take(got_slope, layer_slot, axis=1)
    updated = particle(shell_conc[0], kelvin[0], layer_current[0])[None]
    own_live = lax.dynamic_slice_in_dim(live_slot, position * slot_count, slot_count)
    conc_new = jnp.where(own_live[None, :, None, None, None], updated, 0.0)
    face_rows = jnp.stack([heat_rise[:, 0], heat_rise[:, layer_total - 1]], axis=1)
    every_face = lax.all_gather(face_rows, "cell", axis=0, tiled=True)
    partners = lax.dynamic_index_in_dim(contacts, lax.axis_index("cell"), 0, keepdims=False)
    lower_pair = lax.dynamic_index_in_dim(
        every_face, jnp.maximum(partners[0], 0), 0, keepdims=False
    )
    upper_pair = lax.dynamic_index_in_dim(
        every_face, jnp.maximum(partners[1], 0), 0, keepdims=False
    )
    below_face = jnp.where(partners[0] >= 0, lower_pair[1], 0.0)[None]
    above_face = jnp.where(partners[1] >= 0, upper_pair[0], 0.0)[None]
    rim_rows = with_halo(heat_rise, (("sub", 2),), 1)
    low_row = jnp.where(position == 0, heat_rise[:, :, 0:1], rim_rows[:, :, 0:1])
    high_row = jnp.where(position == devices - 1, heat_rise[:, :, -1:], rim_rows[:, :, -1:])
    column_pad = jnp.concatenate([low_row, heat_rise, high_row], axis=2)
    row_pad = jnp.pad(heat_rise, ((0, 0), (0, 0), (0, 0), (1, 1)), mode="edge")
    laplace = (
        column_pad[:, :, 2:]
        + column_pad[:, :, :-2]
        + row_pad[:, :, :, 2:]
        + row_pad[:, :, :, :-2]
        - 4.0 * heat_rise
    )
    right_side = heat_rise + INPLANE_CONDUCT * laplace + layer_source - layer_slope * heat_rise
    first_row = right_side[:, 0] + CONTACT_CONDUCT * (below_face - heat_rise[:, 0])
    last_row = right_side[:, layer_total - 1] + CONTACT_CONDUCT * (
        above_face - heat_rise[:, layer_total - 1]
    )
    right_side = jnp.concatenate(
        [first_row[:, None], right_side[:, 1 : layer_total - 1], last_row[:, None]], axis=1
    )
    heat_new = column_solve(right_side, layer_slope)
    return (conc_new, heat_new)


def solution(mesh):
    in_specs = (
        P("cell", "sub", None, None, None),
        P("cell", None, "sub", None),
        P("cell", "sub", None, None),
        P(),
        P(),
    )
    out_specs = (P("cell", "sub", None, None, None), P("cell", None, "sub", None))
    return jax.shard_map(
        per_device, mesh=mesh, in_specs=in_specs, out_specs=out_specs, check_vma=False
    )
```

profile of v0, /device:TPU:0, one launch (start us, length us, event | category | flops | bytes accessed | tf_op | source)
XLA Modules:
  0.0 71.9 jit_solution(17056215816559929877)
XLA Ops:
  0.6 1.0 %fusion.193 = (f32[1,30,1,128]{3,2,1,0:T(1,128)S(1)}, f32[1,30,1,128]{3,2,1,0:T(1,128)S(1)}) fusion(f32[1,30,16,128]{3,2,1,0:T(8,128)} %param.8), kind=kLoop, calls=%fused_computation.427 | loop fusion | bytes 61440 | tf_op jit(solution)/shard_map/slice | solution.py:176
  1.6 1.3 %collective-permute-start = (f32[1,30,1,128]{3,2,1,0:T(1,128)S(1)}, f32[1,30,1,128]{3,2,1,0:T(1,128)S(1)}, u32[]{:S(2)}, u32[]{:S(2)}) collective-permute-start(f32[1,30,1,128]{3,2,1,0:T(1,128)S(1)} %get-tuple-element.86), channel_id=1, source_target_pairs={{1,0},{2,1},{3,2},{4,3},{5,4},{6,5},{7,6},{9,8},{10,9},{11,10},{12... | collective-permute-start | bytes 46088 | tf_op jit(solution)/shard_map/ppermute | solution.py:30
  2.9 3.0 %collective-permute-start.1 = (f32[1,30,1,128]{3,2,1,0:T(1,128)S(1)}, f32[1,30,1,128]{3,2,1,0:T(1,128)S(1)}, u32[]{:S(2)}, u32[]{:S(2)}) collective-permute-start(f32[1,30,1,128]{3,2,1,0:T(1,128)S(1)} %get-tuple-element.87), channel_id=1, source_target_pairs={{0,1},{1,2},{2,3},{3,4},{4,5},{5,6},{6,7},{8,9},{9,10},{10,11},{11... | collective-permute-start | bytes 46088 | tf_op jit(solution)/shard_map/ppermute | solution.py:28
  6.0 0.8 %reduce-window.8 = s32[8,1]{0,1:T(1,128)S(1)} reduce-window(s32[8,1]{0,1:T(1,128)} %bitcast.460, s32[]{:T(128)} %constant.160.clone.1), window={size=8x1 pad=7_0x0_0}, to_apply=%region_1.2 | reduce-window | flops 56 | bytes 68 | tf_op jit(solution)/shard_map/reduce-window.3
  7.5 0.7 %select_reduce_fusion.2 = (s32[32]{0:T(128)S(1)}, s32[32]{0:T(128)S(1)}) fusion(s32[8]{0:T(128)} %param.10, s32[32]{0:T(128)S(1)} %and_select_fusion.1, s32[8]{0:T(128)S(1)} %bitcast_subtract_fusion), kind=kLoop, calls=%fused_computation.407 | loop fusion | flops 1216 | bytes 448 | tf_op jit(solution)/shard_map/reduce_sum | solution.py:53
  8.3 1.5 %gather_fusion = f32[32,16,128]{2,1,0:T(8,128)S(1)} fusion(f32[30,16,128]{2,1,0:T(8,128)} %bitcast.445, s32[1024]{0:T(1024)S(1)} %pad_clamp_fusion.1), kind=kCustom, calls=%fused_computation.2 | custom fusion | bytes 524416 | tf_op jit(solution)/shard_map/jit(_take)/gather | solution.py:150
  9.8 0.8 %bitcast_select_fusion = f32[1,32,16,128]{3,2,0,1:T(8,128)} fusion(f32[32,16,128]{2,1,0:T(8,128)S(1)} %gather_fusion, pred[32]{0:T(512)(128)(4,1)S(1)} %compare_and_fusion.1), kind=kLoop, calls=%fused_computation.119 | loop fusion | flops 65536 | bytes 524320 | tf_op jit(solution)/shard_map/jit(_take)/select_n | solution.py:150
  10.6 6.4 %all-to-all-start = ((f32[1,32,16,128]{3,2,0,1:T(8,128)}), f32[1,32,16,128]{3,2,0,1:T(8,128)S(1)}, u32[]{:S(2)}, u32[]{:S(2)}) async-start(f32[1,32,16,128]{3,2,0,1:T(8,128)} %bitcast_select_fusion), calls=%async_computation | async-start | bytes 524288 | tf_op jit(solution)/shard_map/all_to_all | solution.py:151
  17.7 1.9 %fusion.194 = (f32[1,30,16,1]{3,2,1,0:T(8,128)}, f32[1,30,16,1]{3,2,1,0:T(8,128)}) fusion(f32[1,30,16,128]{3,2,1,0:T(8,128)} %param.8), kind=kLoop, calls=%fused_computation.428 | loop fusion | bytes 7680 | tf_op jit(solution)/shard_map/jit(_pad)/slice | solution.py:179
  22.9 2.0 %copy.155 = f32[1,4,10,128,128]{4,3,1,2,0:T(8,128)S(1)} copy(f32[1,4,10,128,128]{4,3,2,1,0:T(8,128)} %param.7) | data formatting | bytes 5242880 | tf_op args[0]
  25.0 8.2 %all_gather.3 = f32[4,2,16,128]{3,2,1,0:T(8,128)S(1)} all-gather(f32[1,2,16,128]{3,2,1,0:T(8,128)S(1)} %pad_maximum_fusion.4), channel_id=1, replica_groups=mesh['cell'=4,'sub'=8] {'cell'}, dimensions={0}, use_global_device_ids=true | all-gather | bytes 81920 | tf_op jit(solution)/shard_map/all_gather | solution.py:165
  35.8 0.7 %copy.132 = f32[1,4,8,16,128]{4,3,2,1,0:T(8,128)} copy(f32[1,4,8,16,128]{4,3,1,2,0:T(8,128)S(1)} %bitcast.451) | data formatting | bytes 524288 | tf_op jit(solution)/shard_map/mul | solution.py:95
  36.5 0.7 %copy.133 = f32[1,4,8,16,128]{4,3,2,1,0:T(8,128)} copy(f32[1,4,8,16,128]{4,3,1,2,0:T(8,128)S(1)} %bitcast.450) | data formatting | bytes 524288 | tf_op jit(solution)/shard_map/mul | solution.py:95
  38.7 1.3 %fusion.33 = (f32[1,4,128,128]{3,2,1,0:T(8,128)S(1)}, f32[1,4,128,128]{3,2,1,0:T(8,128)}) fusion(f32[1,8,4,16,128]{4,3,1,2,0:T(8,128)S(1)} %copy.145, f32[1,4,128,128]{3,2,1,0:T(8,128)S(1)} %copy-done.9, f32[1,4,10,128,128]{4,3,1,2,0:T(8,128)S(1)} %copy.155), kind=kLoop, calls=%fused_computation.65 | loop fusion | flops 2162688 | bytes 1310720 | tf_op jit(solution)/shard_map/mul | solution.py:76
  39.9 0.9 %copy.150 = f32[1,4,128,128]{3,1,0,2:T(4,128)} copy(f32[1,4,128,128]{3,2,1,0:T(8,128)S(1)} %get-tuple-element.66) | data formatting | bytes 524288 | tf_op jit(solution)/shard_map/mul | solution.py:76
  40.8 5.1 %all-to-all-start.2 = ((f32[1,4,128,128]{3,1,0,2:T(4,128)}), f32[1,4,128,128]{3,1,0,2:T(4,128)}, u32[]{:S(2)}, u32[]{:S(2)}) async-start(f32[1,4,128,128]{3,1,0,2:T(4,128)} %copy.150), calls=%async_computation.2 | async-start | bytes 524288 | tf_op jit(solution)/shard_map/all_to_all | solution.py:157
  45.9 1.8 %copy.147 = f32[1,4,128,128]{3,1,0,2:T(4,128)} copy(f32[1,4,128,128]{3,2,1,0:T(8,128)} %get-tuple-element.67) | data formatting | bytes 524288 | tf_op jit(solution)/shard_map/mul | solution.py:74
  47.8 2.2 %fusion.10 = (f32[4,1,128,128]{3,2,0,1:T(8,128)S(1)}, f32[4,1,128,128]{3,2,0,1:T(8,128)S(1)}, f32[4,1,128,128]{3,2,0,1:T(8,128)S(1)}, f32[4,1,128,128]{3,2,0,1:T...) fusion(f32[4,10,128,128]{3,2,0,1:T(8,128)S(1)} %bitcast.443, ...), kind=kLoop, calls=%fused_computation.22 | loop fusion | flops 4325376 | bytes 7077888 | tf_op jit(solution)/shard_map/div | solution.py:114
  51.5 4.2 %all-to-all-done.2 = f32[1,4,128,128]{3,1,0,2:T(4,128)} async-done(((f32[1,4,128,128]{3,1,0,2:T(4,128)}), f32[1,4,128,128]{3,1,0,2:T(4,128)}, u32[]{:S(2)}, u32[]{:S(2)}) %all-to-all-start.2) | async-done | bytes 262176 | tf_op jit(solution)/shard_map/all_to_all | solution.py:157
  55.7 3.4 %all-to-all-start.1 = ((f32[1,4,128,128]{3,1,0,2:T(4,128)}), f32[1,4,128,128]{3,1,0,2:T(4,128)S(1)}, u32[]{:S(2)}, u32[]{:S(2)}) async-start(f32[1,4,128,128]{3,1,0,2:T(4,128)} %copy.147), calls=%async_computation.1 | async-start | bytes 524288 | tf_op jit(solution)/shard_map/all_to_all | solution.py:156
  59.1 1.0 %bitcast_dynamic-update-slice_fusion.9 = f32[1,4,10,128,128]{4,3,2,1,0:T(8,128)S(1)} fusion(f32[1,4,10,128,128]{4,3,2,1,0:T(8,128)S(1)} %bitcast_dynamic-update-slice_fusion, f32[4,1,128,128]{3,2,0,1:T(8,128)} %copy-done.8), kind=kLoop, calls=%fused_computation.66 | loop fusion | bytes 524288 | tf_op jit(solution)/shard_map/stack | solution.py:119
  60.1 1.8 %broadcast_select_fusion = f32[1,4,10,128,128]{4,3,2,1,0:T(8,128)} fusion(f32[1,4,10,128,128]{4,3,2,1,0:T(8,128)S(1)} %bitcast_dynamic-update-slice_fusion.9, pred[4]{0:T(512)(128)(4,1)S(1)} %dynamic_slice.14), kind=kLoop, calls=%fused_computation.3 | loop fusion | flops 655360 | bytes 5242884 | tf_op jit(solution)/shard_map/jit(_where)/select_n | solution.py:163
  62.0 1.0 %copy.151 = f32[1,4,128,128]{3,2,1,0:T(8,128)S(1)} copy(f32[1,4,128,128]{3,1,0,2:T(4,128)} %all-to-all-done.2) | data formatting | bytes 524288 | tf_op jit(solution)/shard_map/all_to_all | solution.py:157
  63.0 5.8 %all-to-all-done.1 = f32[1,4,128,128]{3,1,0,2:T(4,128)S(1)} async-done(((f32[1,4,128,128]{3,1,0,2:T(4,128)}), f32[1,4,128,128]{3,1,0,2:T(4,128)S(1)}, u32[]{:S(2)}, u32[]{:S(2)}) %all-to-all-start.1) | async-done | bytes 262176 | tf_op jit(solution)/shard_map/all_to_all | solution.py:156
  (104 shorter events, 10.5 us)
Async XLA Ops:
  0.6 19.1 %copy-start = (s32[4,2]{0,1:T(2,128)S(1)}, s32[4,2]{0,1:T(2,128)}, u32[]{:S(2)}) copy-start(s32[4,2]{0,1:T(2,128)} %param.11) | copy-start | bytes 100
  1.6 31.6 %collective-permute-start = (f32[1,30,1,128]{3,2,1,0:T(1,128)S(1)}, f32[1,30,1,128]{3,2,1,0:T(1,128)S(1)}, u32[]{:S(2)}, u32[]{:S(2)}) collective-permute-start(f32[1,30,1,128]{3,2,1,0:T(1,128)S(1)} %get-tuple-element.86), channel_id=1, source_target_pairs={{1,0},{2,1},{3,2},{4,3},{5,4},{6,5},{7,6},{9,8},{10,9},{11,10},{12... | collective-permute-start | bytes 46088 | tf_op jit(solution)/shard_map/ppermute | solution.py:30
  2.9 30.3 %collective-permute-start.1 = (f32[1,30,1,128]{3,2,1,0:T(1,128)S(1)}, f32[1,30,1,128]{3,2,1,0:T(1,128)S(1)}, u32[]{:S(2)}, u32[]{:S(2)}) collective-permute-start(f32[1,30,1,128]{3,2,1,0:T(1,128)S(1)} %get-tuple-element.87), channel_id=1, source_target_pairs={{0,1},{1,2},{2,3},{3,4},{4,5},{5,6},{6,7},{8,9},{9,10},{10,11},{11... | collective-permute-start | bytes 46088 | tf_op jit(solution)/shard_map/ppermute | solution.py:28
  10.6 22.7 %all-to-all-start = ((f32[1,32,16,128]{3,2,0,1:T(8,128)}), f32[1,32,16,128]{3,2,0,1:T(8,128)S(1)}, u32[]{:S(2)}, u32[]{:S(2)}) async-start(f32[1,32,16,128]{3,2,0,1:T(8,128)} %bitcast_select_fusion), calls=%async_computation | async-start | bytes 524288 | tf_op jit(solution)/shard_map/all_to_all | solution.py:151
  22.9 10.3 %copy-start.1 = (f32[1,30,16,128]{3,2,1,0:T(8,128)S(1)}, f32[1,30,16,128]{3,2,1,0:T(8,128)}, u32[]{:S(2)}) copy-start(f32[1,30,16,128]{3,2,1,0:T(8,128)} %param.8) | copy-start | bytes 737284
  33.6 5.1 %copy-start.9 = (f32[1,4,128,128]{3,2,1,0:T(8,128)S(1)}, f32[1,4,128,128]{3,2,1,0:T(8,128)}, u32[]{:S(2)}) copy-start(f32[1,4,128,128]{3,2,1,0:T(8,128)} %param.9) | copy-start | bytes 786436
  40.8 14.9 %all-to-all-start.2 = ((f32[1,4,128,128]{3,1,0,2:T(4,128)}), f32[1,4,128,128]{3,1,0,2:T(4,128)}, u32[]{:S(2)}, u32[]{:S(2)}) async-start(f32[1,4,128,128]{3,1,0,2:T(4,128)} %copy.150), calls=%async_computation.2 | async-start | bytes 524288 | tf_op jit(solution)/shard_map/all_to_all | solution.py:157
  47.7 2.3 %copy-start.2 = (f32[1,4,8,16,128]{4,3,2,1,0:T(8,128)S(1)}, f32[1,4,8,16,128]{4,3,2,1,0:T(8,128)}, u32[]{:S(2)}) copy-start(f32[1,4,8,16,128]{4,3,2,1,0:T(8,128)} %copy.129) | copy-start | bytes 786436
  47.7 2.3 %copy-start.3 = (f32[1,4,8,16,128]{4,3,2,1,0:T(8,128)S(1)}, f32[1,4,8,16,128]{4,3,2,1,0:T(8,128)}, u32[]{:S(2)}) copy-start(f32[1,4,8,16,128]{4,3,2,1,0:T(8,128)} %copy.130) | copy-start | bytes 786436
  47.7 2.3 %copy-start.4 = (f32[1,4,8,16,128]{4,3,2,1,0:T(8,128)S(1)}, f32[1,4,8,16,128]{4,3,2,1,0:T(8,128)}, u32[]{:S(2)}) copy-start(f32[1,4,8,16,128]{4,3,2,1,0:T(8,128)} %copy.131) | copy-start | bytes 786436
  47.7 2.3 %copy-start.5 = (f32[1,4,8,16,128]{4,3,2,1,0:T(8,128)S(1)}, f32[1,4,8,16,128]{4,3,2,1,0:T(8,128)}, u32[]{:S(2)}) copy-start(f32[1,4,8,16,128]{4,3,2,1,0:T(8,128)} %copy.132) | copy-start | bytes 786436
  47.7 2.3 %copy-start.6 = (f32[1,4,8,16,128]{4,3,2,1,0:T(8,128)S(1)}, f32[1,4,8,16,128]{4,3,2,1,0:T(8,128)}, u32[]{:S(2)}) copy-start(f32[1,4,8,16,128]{4,3,2,1,0:T(8,128)} %copy.133) | copy-start | bytes 786436
  47.8 2.3 %copy-start.7 = (f32[1,4,8,16,128]{4,3,2,1,0:T(8,128)S(1)}, f32[1,4,8,16,128]{4,3,2,1,0:T(8,128)}, u32[]{:S(2)}) copy-start(f32[1,4,8,16,128]{4,3,2,1,0:T(8,128)} %copy.134) | copy-start | bytes 786436
  47.8 2.3 %copy-start.10 = (f32[1,4,128,128]{3,2,1,0:T(8,128)S(1)}, f32[1,4,128,128]{3,2,1,0:T(8,128)}, u32[]{:S(2)}) copy-start(f32[1,4,128,128]{3,2,1,0:T(8,128)} %param.9) | copy-start | bytes 786436
  47.8 2.3 %copy-start.11 = (f32[1,4,8,16,128]{4,3,2,1,0:T(8,128)S(1)}, f32[1,4,8,16,128]{4,3,2,1,0:T(8,128)}, u32[]{:S(2)}) copy-start(f32[1,4,8,16,128]{4,3,2,1,0:T(8,128)} %copy.135) | copy-start | bytes 786436
  50.7 0.7 copy-start.8
  55.7 13.1 %all-to-all-start.1 = ((f32[1,4,128,128]{3,1,0,2:T(4,128)}), f32[1,4,128,128]{3,1,0,2:T(4,128)S(1)}, u32[]{:S(2)}, u32[]{:S(2)}) async-start(f32[1,4,128,128]{3,1,0,2:T(4,128)} %copy.147), calls=%async_computation.1 | async-start | bytes 524288 | tf_op jit(solution)/shard_map/all_to_all | solution.py:156
  62.0 8.1 %copy-start.12 = (f32[1,30,16,1]{3,2,1,0:T(8,128)S(1)}, f32[1,30,16,1]{3,2,1,0:T(8,128)}, u32[]{:S(2)}) copy-start(f32[1,30,16,1]{3,2,1,0:T(8,128)} %get-tuple-element.88) | copy-start | bytes 5764
  62.0 8.1 %copy-start.13 = (f32[1,30,16,1]{3,2,1,0:T(8,128)S(1)}, f32[1,30,16,1]{3,2,1,0:T(8,128)}, u32[]{:S(2)}) copy-start(f32[1,30,16,1]{3,2,1,0:T(8,128)} %get-tuple-element.89) | copy-start | bytes 5764
  71.2 0.7 copy-start.14
where the time goes:
time: 72.6 us; the launch traced here: 71.9 us
  local copies, waits for them, and re-layouts  20 us (28%)
  starting transfers between devices  19.2 us (26%)
  other arithmetic  10.6 us (15%)
  waiting for transfers between devices  10 us (14%)
  blocking collectives  8.23 us (11%)
  between operations  3.8 us (5%)
    all_gather x1, blocking collectives, per_device(): every_face = lax.all_gather(face_rows, 'cell', axis=0, tiled=True)  8.23 us
    all_to_all x1, starting transfers between devices, per_device(): lax.all_to_all(outgoing, 'sub', split_axis=1, concat_axis=2, tiled=True)  6.35 us
    all_to_all x1, waiting for transfers between devices, per_device(): lax.all_to_all(source, 'sub', split_axis=2, concat_axis=1, tiled=True)  5.76 us
    all_to_all x1, starting transfers between devices, per_device(): lax.all_to_all(heat_slope, 'sub', split_axis=2, concat_axis=1, tiled=True)  5.1 us
    mul x9, local copies, waits for them, and re-layouts, particle(): DIFFUSION_STEP * speedup * ((radial + 1) ** 2 / shells ** 2 * shells)  5.07 us
    all_to_all x1, waiting for transfers between devices, per_device(): lax.all_to_all(heat_slope, 'sub', split_axis=2, concat_axis=1, tiled=True)  4.23 us
    all_to_all x1, starting transfers between devices, per_device(): lax.all_to_all(source, 'sub', split_axis=2, concat_axis=1, tiled=True)  3.41 us
    unnamed x50, local copies, waits for them, and re-layouts  3.22 us
  transfers between devices with their start and end apart: 5, of which 2 were waited for; matrix products, arithmetic and copies ran while one was open for 26% of the time, Pallas kernels for 0%

commit v1 on v0

--- a/solution.py
+++ b/solution.py
@@ -15,6 +15,12 @@
 INPLANE_CONDUCT = 0.25
 THROUGH_CONDUCT = 2.0
 CONTACT_CONDUCT = 0.5
+
+
+def trade_parts(x, axis, split, join):
+    pieces = jnp.split(x, lax.axis_size(axis), axis=split)
+    received = lax.all_to_all(jnp.stack(pieces), axis, 0, 0)
+    return jnp.concatenate(received, axis=join)
 
 
 def with_halo(cells, sides, width):
@@ -154,7 +160,7 @@
     source, heat_slope = kinetics(surface, kelvin, layer_current)
     got_source, got_slope = (
         lax.all_to_all(source, "sub", split_axis=2, concat_axis=1, tiled=True),
-        lax.all_to_all(heat_slope, "sub", split_axis=2, concat_axis=1, tiled=True),
+        trade_parts(heat_slope, "sub", 2, 1),
     )
     layer_source = jnp.take(got_source, layer_slot, axis=1)
     layer_slope = jnp.take(got_slope, layer_slot, axis=1)

time: 72.6 us -> 75.8 us (1.044)
  waiting for transfers between devices: 10 us -> 5.2 us
  local copies, waits for them, and re-layouts: 20 us -> 24.7 us
  starting transfers between devices: 19.2 us -> 20.9 us
  other arithmetic: 10.6 us -> 11.6 us
    unnamed x50 -> x57, local copies, waits for them, and re-layouts: 3.22 us -> 8.99 us
    all_to_all x1, waiting for transfers between devices: 5.76 us -> 0.01 us  [per_device(): lax.all_to_all(source, 'sub', split_axis=2, concat_axis=1, tiled=True)]
    all_to_all x1, starting transfers between devices: 3.41 us -> 5.1 us  [per_device(): lax.all_to_all(source, 'sub', split_axis=2, concat_axis=1, tiled=True)]
    all_to_all x2 -> x0, local copies, waits for them, and re-layouts: 1.04 us -> none  [per_device(): lax.all_to_all(heat_slope, 'sub', split_axis=2, concat_axis=1, tiled=True)]
    mul x1, local copies, waits for them, and re-layouts: 1.82 us -> 0.86 us  [kinetics(): source = HEAT_SCALE * current * (overvoltage + kelvin * entropic)]
    all_to_all x1, waiting for transfers between devices: 4.23 us -> 5.18 us  [trade_parts(): received = lax.all_to_all(jnp.stack(pieces), axis, 0, 0)]
    all_to_all x2, local copies, waits for them, and re-layouts: 0.04 us -> 0.99 us  [per_device(): lax.all_to_all(source, 'sub', split_axis=2, concat_axis=1, tiled=True)]
    select_n x1, other arithmetic: 0.32 us -> 1.25 us  [per_device(): layer_slope = jnp.take(got_slope, layer_slot, axis=1)]
  transfers between devices with their start and end apart: 5 -> 5, of which waited for: 2 -> 1; matrix products, arithmetic and copies ran while one was open for 26% -> 32% of each run, Pallas kernels for 0% -> 0%
where the time goes in v1:
time: 75.8 us; the launch traced here: 74.4 us
  local copies, waits for them, and re-layouts  24.7 us (33%)
  starting transfers between devices  20.9 us (28%)
  other arithmetic  11.6 us (15%)
  blocking collectives  8.23 us (11%)
  waiting for transfers between devices  5.2 us (7%)
  between operations  3.81 us (5%)
    unnamed x57, local copies, waits for them, and re-layouts  8.99 us
    all_gather x1, blocking collectives, per_device(): every_face = lax.all_gather(face_rows, 'cell', axis=0, tiled=True)  8.23 us
    all_to_all x1, starting transfers between devices, per_device(): lax.all_to_all(outgoing, 'sub', split_axis=1, concat_axis=2, tiled=True)  6.35 us
    all_to_all x1, waiting for transfers between devices, trade_parts(): received = lax.all_to_all(jnp.stack(pieces), axis, 0, 0)  5.18 us
    all_to_all x1, starting transfers between devices, trade_parts(): received = lax.all_to_all(jnp.stack(pieces), axis, 0, 0)  5.11 us
    all_to_all x1, starting transfers between devices, per_device(): lax.all_to_all(source, 'sub', split_axis=2, concat_axis=1, tiled=True)  5.1 us
    mul x9, local copies, waits for them, and re-layouts, particle(): DIFFUSION_STEP * speedup * ((radial + 1) ** 2 / shells ** 2 * shells)  5.08 us
    ppermute x1, starting transfers between devices, with_halo(): lax.ppermute(tail, axis, [(i, (i + 1) % count) for i in range(ends)])  3.03 us
  transfers between devices with their start and end apart: 5, of which 1 were waited for; matrix products, arithmetic and copies ran while one was open for 32% of the time, Pallas kernels for 0%

profile of v1, /device:TPU:0, one launch (start us, length us, event | category | flops | bytes accessed | tf_op | source)
XLA Modules:
  0.0 74.4 jit_solution(6996664453415383814)
XLA Ops:
  0.6 1.0 %fusion.193 = (f32[1,30,1,128]{3,2,1,0:T(1,128)S(1)}, f32[1,30,1,128]{3,2,1,0:T(1,128)S(1)}) fusion(f32[1,30,16,128]{3,2,1,0:T(8,128)} %param.8), kind=kLoop, calls=%fused_computation.443 | loop fusion | bytes 61440 | tf_op jit(solution)/shard_map/slice | solution.py:182
  1.6 1.3 %collective-permute-start = (f32[1,30,1,128]{3,2,1,0:T(1,128)S(1)}, f32[1,30,1,128]{3,2,1,0:T(1,128)S(1)}, u32[]{:S(2)}, u32[]{:S(2)}) collective-permute-start(f32[1,30,1,128]{3,2,1,0:T(1,128)S(1)} %get-tuple-element.86), channel_id=1, source_target_pairs={{1,0},{2,1},{3,2},{4,3},{5,4},{6,5},{7,6},{9,8},{10,9},{11,10},{12... | collective-permute-start | bytes 46088 | tf_op jit(solution)/shard_map/ppermute | solution.py:36
  2.9 3.0 %collective-permute-start.1 = (f32[1,30,1,128]{3,2,1,0:T(1,128)S(1)}, f32[1,30,1,128]{3,2,1,0:T(1,128)S(1)}, u32[]{:S(2)}, u32[]{:S(2)}) collective-permute-start(f32[1,30,1,128]{3,2,1,0:T(1,128)S(1)} %get-tuple-element.87), channel_id=1, source_target_pairs={{0,1},{1,2},{2,3},{3,4},{4,5},{5,6},{6,7},{8,9},{9,10},{10,11},{11... | collective-permute-start | bytes 46088 | tf_op jit(solution)/shard_map/ppermute | solution.py:34
  6.0 0.8 %reduce-window.8 = s32[8,1]{0,1:T(1,128)S(1)} reduce-window(s32[8,1]{0,1:T(1,128)} %bitcast.488, s32[]{:T(128)} %constant.160.clone.1), window={size=8x1 pad=7_0x0_0}, to_apply=%region_1.2 | reduce-window | flops 56 | bytes 68 | tf_op jit(solution)/shard_map/reduce-window.3
  8.3 1.5 %gather_fusion = f32[32,16,128]{2,1,0:T(8,128)S(1)} fusion(f32[30,16,128]{2,1,0:T(8,128)} %bitcast.474, s32[1024]{0:T(1024)S(1)} %pad_clamp_fusion.1), kind=kCustom, calls=%fused_computation.2 | custom fusion | bytes 524416 | tf_op jit(solution)/shard_map/jit(_take)/gather | solution.py:156
  9.8 0.8 %bitcast_select_fusion = f32[1,32,16,128]{3,2,0,1:T(8,128)} fusion(f32[32,16,128]{2,1,0:T(8,128)S(1)} %gather_fusion, pred[32]{0:T(512)(128)(4,1)S(1)} %compare_and_fusion.1), kind=kLoop, calls=%fused_computation.119 | loop fusion | flops 65536 | bytes 524320 | tf_op jit(solution)/shard_map/jit(_take)/select_n | solution.py:156
  10.6 6.4 %all-to-all-start = ((f32[1,32,16,128]{3,2,0,1:T(8,128)}), f32[1,32,16,128]{3,2,0,1:T(8,128)S(1)}, u32[]{:S(2)}, u32[]{:S(2)}) async-start(f32[1,32,16,128]{3,2,0,1:T(8,128)} %bitcast_select_fusion), calls=%async_computation | async-start | bytes 524288 | tf_op jit(solution)/shard_map/all_to_all | solution.py:157
  17.7 1.9 %fusion.194 = (f32[1,30,16,1]{3,2,1,0:T(8,128)}, f32[1,30,16,1]{3,2,1,0:T(8,128)}) fusion(f32[1,30,16,128]{3,2,1,0:T(8,128)} %param.8), kind=kLoop, calls=%fused_computation.444 | loop fusion | bytes 7680 | tf_op jit(solution)/shard_map/jit(_pad)/slice | solution.py:185
  22.9 2.1 %copy.226 = f32[1,4,10,128,128]{4,3,1,2,0:T(8,128)S(1)} copy(f32[1,4,10,128,128]{4,3,2,1,0:T(8,128)} %param.7) | data formatting | bytes 5242880 | tf_op args[0]
  25.1 8.2 %all_gather.3 = f32[4,2,16,128]{3,2,1,0:T(8,128)S(1)} all-gather(f32[1,2,16,128]{3,2,1,0:T(8,128)S(1)} %pad_maximum_fusion.4), channel_id=1, replica_groups=mesh['cell'=4,'sub'=8] {'cell'}, dimensions={0}, use_global_device_ids=true | all-gather | bytes 81920 | tf_op jit(solution)/shard_map/all_gather | solution.py:171
  38.8 1.3 %fusion.33 = (f32[1,4,128,128]{3,2,1,0:T(8,128)}, f32[1,4,128,128]{3,2,1,0:T(8,128)S(1)}) fusion(f32[1,8,4,16,128]{4,3,1,2,0:T(8,128)S(1)} %copy.219, f32[1,4,128,128]{3,2,1,0:T(8,128)S(1)} %copy-done.9, f32[1,4,10,128,128]{4,3,1,2,0:T(8,128)S(1)} %copy.226), kind=kLoop, calls=%fused_computation.65 | loop fusion | flops 2162688 | bytes 1310720 | tf_op jit(solution)/shard_map/mul | solution.py:82
  40.1 0.9 %copy.221 = f32[1,4,128,128]{3,1,0,2:T(4,128)} copy(f32[1,4,128,128]{3,2,1,0:T(8,128)S(1)} %get-tuple-element.67) | data formatting | bytes 524288 | tf_op jit(solution)/shard_map/mul | solution.py:80
  40.9 5.1 %all-to-all-start.1 = ((f32[1,4,128,128]{3,1,0,2:T(4,128)}), f32[1,4,128,128]{3,1,0,2:T(4,128)}, u32[]{:S(2)}, u32[]{:S(2)}) async-start(f32[1,4,128,128]{3,1,0,2:T(4,128)} %copy.221), calls=%async_computation.1 | async-start | bytes 524288 | tf_op jit(solution)/shard_map/all_to_all | solution.py:162
  46.8 0.8 %constant_dynamic-update-slice_fusion.6 = f32[8,1,4,16,128]{4,3,2,1,0:T(8,128)S(1)} fusion(f32[8,1,4,16,128]{4,3,2,1,0:T(8,128)S(1)} %constant_dynamic-update-slice_fusion.7, f32[1,4,128,128]{3,2,1,0:T(8,128)} %get-tuple-element.66), kind=kLoop, calls=%fused_computation.162 | loop fusion | bytes 65536
  47.5 0.8 %constant_dynamic-update-slice_fusion.5 = f32[8,1,4,16,128]{4,3,2,1,0:T(8,128)S(1)} fusion(f32[8,1,4,16,128]{4,3,2,1,0:T(8,128)S(1)} %constant_dynamic-update-slice_fusion.6, f32[1,4,128,128]{3,2,1,0:T(8,128)} %get-tuple-element.66), kind=kLoop, calls=%fused_computation.161 | loop fusion | bytes 65536
  50.6 0.8 %constant_dynamic-update-slice_fusion.1 = f32[8,1,4,16,128]{4,3,2,1,0:T(8,128)S(1)} fusion(f32[8,1,4,16,128]{4,3,2,1,0:T(8,128)S(1)} %constant_dynamic-update-slice_fusion.2, f32[1,4,128,128]{3,2,1,0:T(8,128)} %get-tuple-element.66), kind=kLoop, calls=%fused_computation.157 | loop fusion | bytes 65536
  51.4 2.2 %fusion.10 = (f32[4,1,128,128]{3,2,0,1:T(8,128)S(1)}, f32[4,1,128,128]{3,2,0,1:T(8,128)S(1)}, f32[4,1,128,128]{3,2,0,1:T(8,128)S(1)}, f32[4,1,128,128]{3,2,0,1:T...) fusion(f32[4,10,128,128]{3,2,0,1:T(8,128)S(1)} %bitcast.472, ...), kind=kLoop, calls=%fused_computation.22 | loop fusion | flops 4325376 | bytes 7077888 | tf_op jit(solution)/shard_map/div | solution.py:120
  54.7 0.8 %constant_dynamic-update-slice_fusion = f32[8,1,4,16,128]{4,3,2,1,0:T(8,128)S(1)} fusion(f32[8,1,4,16,128]{4,3,2,1,0:T(8,128)S(1)} %constant_dynamic-update-slice_fusion.1, f32[1,4,128,128]{3,2,1,0:T(8,128)} %get-tuple-element.66), kind=kLoop, calls=%fused_computation.156 | loop fusion | bytes 65536 | tf_op jit(solution)/shard_map/stack | solution.py:22
  56.2 5.1 %all-to-all-start.2 = ((f32[8,1,4,16,128]{4,3,2,1,0:T(8,128)}), f32[8,1,4,16,128]{4,3,2,1,0:T(8,128)S(1)}, u32[]{:S(2)}, u32[]{:S(2)}) async-start(f32[8,1,4,16,128]{4,3,2,1,0:T(8,128)} %copy-done.13), calls=%async_computation.2 | async-start | bytes 524288 | tf_op jit(solution)/shard_map/all_to_all | solution.py:22
  61.3 1.0 %bitcast_dynamic-update-slice_fusion.9 = f32[1,4,10,128,128]{4,3,2,1,0:T(8,128)S(1)} fusion(f32[1,4,10,128,128]{4,3,2,1,0:T(8,128)S(1)} %bitcast_dynamic-update-slice_fusion, f32[4,1,128,128]{3,2,0,1:T(8,128)} %copy-done.8), kind=kLoop, calls=%fused_computation.66 | loop fusion | bytes 524288 | tf_op jit(solution)/shard_map/stack | solution.py:125
  62.3 2.0 %broadcast_select_fusion = f32[1,4,10,128,128]{4,3,2,1,0:T(8,128)} fusion(f32[1,4,10,128,128]{4,3,2,1,0:T(8,128)S(1)} %bitcast_dynamic-update-slice_fusion.9, pred[4]{0:T(512)(128)(4,1)S(1)} %dynamic_slice.14), kind=kLoop, calls=%fused_computation.3 | loop fusion | flops 655360 | bytes 5242884 | tf_op jit(solution)/shard_map/jit(_where)/select_n | solution.py:169
  64.3 1.0 %copy.222 = f32[1,4,128,128]{3,2,1,0:T(8,128)S(1)} copy(f32[1,4,128,128]{3,1,0,2:T(4,128)} %all-to-all-done.1) | data formatting | bytes 524288 | tf_op jit(solution)/shard_map/all_to_all | solution.py:162
  65.9 5.2 %all-to-all-done.2 = f32[8,1,4,16,128]{4,3,2,1,0:T(8,128)S(1)} async-done(((f32[8,1,4,16,128]{4,3,2,1,0:T(8,128)}), f32[8,1,4,16,128]{4,3,2,1,0:T(8,128)S(1)}, u32[]{:S(2)}, u32[]{:S(2)}) %all-to-all-start.2) | async-done | bytes 262176 | tf_op jit(solution)/shard_map/all_to_all | solution.py:22
  71.7 1.2 %bitcast_select_fusion.1 = (f32[1,30,16,128]{3,2,1,0:T(8,128)S(1)}, f32[1,30,16,128]{3,2,1,0:T(8,128)S(1)}) fusion(f32[30,16,128]{2,1,0:T(8,128)S(1)} %gather_fusion.2, pred[30]{0:T(512)(128)(4,1)S(1)} %get-tuple-element.48, f32[1,30,16,128]{3,2,1,0:T(8,128)S(1)} %copy-done.1, f32[30,16,128]{2,1,0:T(8,128)S(1)} %gather_fusion.1, ...), kind=kLoop, calls=%fused_computation.144 | loop fusion | flops 983040 | bytes 1263390 | tf_op jit(solution)/shard_map/jit(_take)/select_n | solution.py:166
  (109 shorter events, 15.7 us)
Async XLA Ops:
  0.6 19.1 %copy-start = (s32[4,2]{0,1:T(2,128)S(1)}, s32[4,2]{0,1:T(2,128)}, u32[]{:S(2)}) copy-start(s32[4,2]{0,1:T(2,128)} %param.11) | copy-start | bytes 100
  1.6 31.7 %collective-permute-start = (f32[1,30,1,128]{3,2,1,0:T(1,128)S(1)}, f32[1,30,1,128]{3,2,1,0:T(1,128)S(1)}, u32[]{:S(2)}, u32[]{:S(2)}) collective-permute-start(f32[1,30,1,128]{3,2,1,0:T(1,128)S(1)} %get-tuple-element.86), channel_id=1, source_target_pairs={{1,0},{2,1},{3,2},{4,3},{5,4},{6,5},{7,6},{9,8},{10,9},{11,10},{12... | collective-permute-start | bytes 46088 | tf_op jit(solution)/shard_map/ppermute | solution.py:36
  2.9 30.4 %collective-permute-start.1 = (f32[1,30,1,128]{3,2,1,0:T(1,128)S(1)}, f32[1,30,1,128]{3,2,1,0:T(1,128)S(1)}, u32[]{:S(2)}, u32[]{:S(2)}) collective-permute-start(f32[1,30,1,128]{3,2,1,0:T(1,128)S(1)} %get-tuple-element.87), channel_id=1, source_target_pairs={{0,1},{1,2},{2,3},{3,4},{4,5},{5,6},{6,7},{8,9},{9,10},{10,11},{11... | collective-permute-start | bytes 46088 | tf_op jit(solution)/shard_map/ppermute | solution.py:34
  10.6 22.8 %all-to-all-start = ((f32[1,32,16,128]{3,2,0,1:T(8,128)}), f32[1,32,16,128]{3,2,0,1:T(8,128)S(1)}, u32[]{:S(2)}, u32[]{:S(2)}) async-start(f32[1,32,16,128]{3,2,0,1:T(8,128)} %bitcast_select_fusion), calls=%async_computation | async-start | bytes 524288 | tf_op jit(solution)/shard_map/all_to_all | solution.py:157
  22.9 10.4 %copy-start.1 = (f32[1,30,16,128]{3,2,1,0:T(8,128)S(1)}, f32[1,30,16,128]{3,2,1,0:T(8,128)}, u32[]{:S(2)}) copy-start(f32[1,30,16,128]{3,2,1,0:T(8,128)} %param.8) | copy-start | bytes 737284
  33.7 5.1 %copy-start.9 = (f32[1,4,128,128]{3,2,1,0:T(8,128)S(1)}, f32[1,4,128,128]{3,2,1,0:T(8,128)}, u32[]{:S(2)}) copy-start(f32[1,4,128,128]{3,2,1,0:T(8,128)} %param.9) | copy-start | bytes 786436
  40.9 15.3 %all-to-all-start.1 = ((f32[1,4,128,128]{3,1,0,2:T(4,128)}), f32[1,4,128,128]{3,1,0,2:T(4,128)}, u32[]{:S(2)}, u32[]{:S(2)}) async-start(f32[1,4,128,128]{3,1,0,2:T(4,128)} %copy.221), calls=%async_computation.1 | async-start | bytes 524288 | tf_op jit(solution)/shard_map/all_to_all | solution.py:162
  51.4 2.3 %copy-start.2 = (f32[1,4,8,16,128]{4,3,2,1,0:T(8,128)S(1)}, f32[1,4,8,16,128]{4,3,2,1,0:T(8,128)}, u32[]{:S(2)}) copy-start(f32[1,4,8,16,128]{4,3,2,1,0:T(8,128)} %copy.203) | copy-start | bytes 786436
  51.4 2.3 %copy-start.3 = (f32[1,4,8,16,128]{4,3,2,1,0:T(8,128)S(1)}, f32[1,4,8,16,128]{4,3,2,1,0:T(8,128)}, u32[]{:S(2)}) copy-start(f32[1,4,8,16,128]{4,3,2,1,0:T(8,128)} %copy.204) | copy-start | bytes 786436
  51.4 2.3 %copy-start.4 = (f32[1,4,8,16,128]{4,3,2,1,0:T(8,128)S(1)}, f32[1,4,8,16,128]{4,3,2,1,0:T(8,128)}, u32[]{:S(2)}) copy-start(f32[1,4,8,16,128]{4,3,2,1,0:T(8,128)} %copy.205) | copy-start | bytes 786436
  51.4 2.3 %copy-start.5 = (f32[1,4,8,16,128]{4,3,2,1,0:T(8,128)S(1)}, f32[1,4,8,16,128]{4,3,2,1,0:T(8,128)}, u32[]{:S(2)}) copy-start(f32[1,4,8,16,128]{4,3,2,1,0:T(8,128)} %copy.206) | copy-start | bytes 786436
  51.4 2.3 %copy-start.6 = (f32[1,4,8,16,128]{4,3,2,1,0:T(8,128)S(1)}, f32[1,4,8,16,128]{4,3,2,1,0:T(8,128)}, u32[]{:S(2)}) copy-start(f32[1,4,8,16,128]{4,3,2,1,0:T(8,128)} %copy.207) | copy-start | bytes 786436
  51.4 2.3 %copy-start.7 = (f32[1,4,8,16,128]{4,3,2,1,0:T(8,128)S(1)}, f32[1,4,8,16,128]{4,3,2,1,0:T(8,128)}, u32[]{:S(2)}) copy-start(f32[1,4,8,16,128]{4,3,2,1,0:T(8,128)} %copy.208) | copy-start | bytes 786436
  51.4 2.3 %copy-start.10 = (f32[1,4,128,128]{3,2,1,0:T(8,128)S(1)}, f32[1,4,128,128]{3,2,1,0:T(8,128)}, u32[]{:S(2)}) copy-start(f32[1,4,128,128]{3,2,1,0:T(8,128)} %param.9) | copy-start | bytes 786436
  51.4 2.3 %copy-start.11 = (f32[1,4,8,16,128]{4,3,2,1,0:T(8,128)S(1)}, f32[1,4,8,16,128]{4,3,2,1,0:T(8,128)}, u32[]{:S(2)}) copy-start(f32[1,4,8,16,128]{4,3,2,1,0:T(8,128)} %copy.209) | copy-start | bytes 786436
  54.4 1.8 %copy-start.8 = (f32[4,1,128,128]{3,2,0,1:T(8,128)}, f32[4,1,128,128]{3,2,0,1:T(8,128)S(1)}, u32[]{:S(2)}) copy-start(f32[4,1,128,128]{3,2,0,1:T(8,128)S(1)} %get-tuple-element.54) | copy-start | bytes 786436
  55.5 0.7 copy-start.13
  56.2 14.8 %all-to-all-start.2 = ((f32[8,1,4,16,128]{4,3,2,1,0:T(8,128)}), f32[8,1,4,16,128]{4,3,2,1,0:T(8,128)S(1)}, u32[]{:S(2)}, u32[]{:S(2)}) async-start(f32[8,1,4,16,128]{4,3,2,1,0:T(8,128)} %copy-done.13), calls=%async_computation.2 | async-start | bytes 524288 | tf_op jit(solution)/shard_map/all_to_all | solution.py:22
  62.3 9.3 %copy-start.12 = (f32[1,30,16,1]{3,2,1,0:T(8,128)S(1)}, f32[1,30,16,1]{3,2,1,0:T(8,128)}, u32[]{:S(2)}) copy-start(f32[1,30,16,1]{3,2,1,0:T(8,128)} %get-tuple-element.88) | copy-start | bytes 5764
  73.7 0.7 copy-start.14
